TPU v7x, 128 devices: a whole 4x4x4 slice. The times are simulated.
128 devices in a mesh: dp: 16 (over x, y), mp: 8 (over z, core).
Axes of the slice: x: 4, y: 4, z: 4, core: 2. Of those that a mesh axis runs over, the one named last changes fastest.
Arguments:
- patches: bfloat16 [4096, 6144], P('dp', 'mp'), may hold values from -6 to 6
- dest_group: int32 [4096], P('dp'), may hold values from 0 to 15, as said below
- dest_row: int32 [4096], P('dp'), may hold values from 0 to 255, as said below
- segment: int32 [4096], P('dp'), may hold values from 0 to 31, as said below
- ln_gain: float32 [6144], replicated, may hold values from 0.1 to 1.9
- w_qkv: bfloat16 [6144, 3, 3072], P(None, None, 'mp'), may hold values from -0.078125 to 0.078125
- qk_gain: float32 [2, 128], replicated, may hold values from 0.1 to 1.9
- w_out: bfloat16 [6144, 3072], P(None, 'mp'), may hold values from -0.4375 to 0.4375
- cotangent: bfloat16 [4096, 6144], P('dp', 'mp'), may hold values from -6 to 6
Outputs:
- output: bfloat16 [4096, 6144], P('dp', 'mp')
- input_grad: bfloat16 [4096, 6144], P('dp', 'mp')
- qkv_grad: bfloat16 [6144, 3, 3072], P('dp', None, 'mp')
- out_grad: bfloat16 [6144, 3072], P('dp', 'mp')
Inputs may be any that keep to these rules, and one draw needn't show every extreme that they name: The pairs (dest_group, dest_row) of all rows name every row of every group exactly once. The rows of one group send at most 32 rows to any one group, and in every draw some group sends exactly 32 rows to some group. `dest_row`: see dest_group. `segment`: rows of one group with equal numbers are one image and stand in consecutive rows; numbers lie between 0 and 31.
All inputs are finite; a program needn't handle non-finite values.
Results may differ from a plain program's by a relative error of at most 0.024.
Values may be sent and summed in bfloat16 or wider, within the bound.
A program may use at most 192 MiB of HBM per device.

v0:
```python
import math
import jax
import jax.numpy as jnp
from jax import lax
from jax.sharding import PartitionSpec as P

DH = 128


def norm_heads(values, gain):
    center = values - jnp.mean(values, -1, keepdims=True)
    variance = jnp.mean(center * center, -1, keepdims=True)
    return center * lax.rsqrt(variance + 1e-06) * gain


def attend(projected, image_ids, qk_gain):
    row_count = projected.shape[0]
    head_count = projected.shape[2] // DH
    split_heads = projected.reshape(row_count, 3, head_count, DH)
    queries = norm_heads(split_heads[:, 0], qk_gain[0]).astype(jnp.bfloat16)
    keys_normed = norm_heads(split_heads[:, 1], qk_gain[1]).astype(jnp.bfloat16)
    values_bf = split_heads[:, 2].astype(jnp.bfloat16)
    scores = jnp.einsum(
        "qhd,khd->hqk", queries, keys_normed, preferred_element_type=jnp.float32
    ) * DH ** (-0.5)
    same_image = image_ids[:, None] == image_ids[None, :]
    raised = jnp.where(same_image[None], jnp.exp(scores), 0.0)
    weights = (raised / jnp.sum(raised, -1, keepdims=True)).astype(jnp.bfloat16)
    mixed = jnp.einsum("hqk,khd->qhd", weights, values_bf, preferred_element_type=jnp.float32)
    return mixed.reshape(row_count, head_count * DH).astype(jnp.bfloat16)


def contract_rows(left, right):
    return lax.dot_general(
        left, right, (((0,), (0,)), ((), ())), preferred_element_type=jnp.float32
    )


def contract_cols(left, right):
    return lax.dot_general(
        left, right, (((1,), (1,)), ((), ())), preferred_element_type=jnp.float32
    )


def shards(patches, dest_group, dest_row, segment, ln_gain, w_qkv, qk_gain, w_out, cotangent):
    group_rows, part_width = patches.shape
    groups = lax.axis_size("dp")
    slot_size = 2 * group_rows // groups
    full_width, local_width = w_out.shape
    member = (dest_group[:, None] == jnp.arange(groups, dtype=jnp.int32)[None, :]).astype(jnp.int32)
    rank_within = jnp.sum((jnp.cumsum(member, 0) - 1) * member, 1)
    place = dest_group * slot_size + rank_within
    outbox = jnp.zeros((groups * slot_size, part_width), patches.dtype).at[place].set(patches)
    address = jnp.full((groups * slot_size,), group_rows, jnp.int32).at[place].set(dest_row)
    inbox, arrived_at = (
        lax.all_to_all(
            outbox.reshape(groups, slot_size, part_width),
            "dp",
            split_axis=0,
            concat_axis=0,
            tiled=True,
        ),
        lax.all_to_all(
            address.reshape(groups, slot_size), "dp", split_axis=0, concat_axis=0, tiled=True
        ),
    )
    packed = (
        jnp.zeros((group_rows, part_width), patches.dtype)
        .at[arrived_at.reshape(-1)]
        .set(inbox.reshape(-1, part_width), mode="drop")
    )
    whole_rows, whole_cot = (
        lax.all_gather(packed, "mp", axis=1, tiled=True),
        lax.all_gather(cotangent, "mp", axis=1, tiled=True),
    )
    wide = whole_rows.astype(jnp.float32)
    center = wide - jnp.mean(wide, -1, keepdims=True)
    rstd = lax.rsqrt(jnp.mean(center * center, -1, keepdims=True) + 1e-06)
    unit_rows = center * rstd
    normed = (unit_rows * ln_gain).astype(jnp.bfloat16)
    w_flat = w_qkv.reshape(full_width, 3 * local_width)
    projected = jnp.dot(normed, w_flat, preferred_element_type=jnp.float32).reshape(
        group_rows, 3, local_width
    )
    heads_out, backward = jax.vjp(lambda values: attend(values, segment, qk_gain), projected)
    attn = lax.psum_scatter(
        contract_cols(heads_out, w_out).astype(jnp.bfloat16), "mp", scatter_dimension=1, tiled=True
    ).astype(jnp.float32)
    output = (packed.astype(jnp.float32) + attn).astype(jnp.bfloat16)
    d_heads = jnp.dot(whole_cot, w_out, preferred_element_type=jnp.float32).astype(jnp.bfloat16)
    (d_projected,) = backward(d_heads)
    d_proj_bf = d_projected.astype(jnp.bfloat16).reshape(group_rows, 3 * local_width)
    d_part = contract_cols(d_proj_bf, w_flat)
    my_index = lax.axis_index("mp")
    d_normed = lax.psum(d_part.astype(jnp.bfloat16), "mp").astype(jnp.float32)
    d_unit = d_normed * ln_gain
    d_full = rstd * (
        d_unit
        - jnp.mean(d_unit, -1, keepdims=True)
        - unit_rows * jnp.mean(d_unit * unit_rows, -1, keepdims=True)
    )
    d_input = lax.dynamic_slice_in_dim(d_full, my_index * part_width, part_width, 1)
    input_grad = (cotangent.astype(jnp.float32) + d_input).astype(jnp.bfloat16)
    sum_qkv, sum_out = (
        lax.psum_scatter(
            contract_rows(normed, d_proj_bf).astype(jnp.bfloat16),
            "dp",
            scatter_dimension=0,
            tiled=True,
        ).astype(jnp.float32),
        lax.psum_scatter(
            contract_rows(whole_cot, heads_out).astype(jnp.bfloat16),
            "dp",
            scatter_dimension=0,
            tiled=True,
        ).astype(jnp.float32),
    )
    scale_grad = 1.0 / math.sqrt(group_rows * groups)
    qkv_grad = (sum_qkv * scale_grad).reshape(-1, 3, local_width).astype(jnp.bfloat16)
    out_grad = (sum_out * scale_grad).astype(jnp.bfloat16)
    return (output, input_grad, qkv_grad, out_grad)


def solution(mesh):
    placed = (
        P("dp", "mp"),
        P("dp"),
        P("dp"),
        P("dp"),
        P(),
        P(None, None, "mp"),
        P(),
        P(None, "mp"),
        P("dp", "mp"),
    )
    return jax.shard_map(
        shards,
        mesh=mesh,
        in_specs=placed,
        out_specs=(P("dp", "mp"), P("dp", "mp"), P("dp", None, "mp"), P("dp", "mp")),
        check_vma=False,
    )
```

profile of v0, /device:TPU:1, one launch (start us, length us, event | category | flops | bytes accessed | tf_op | source)
XLA Modules:
  0.0 402.0 jit_solution(2269803845035048360)
XLA Ops:
  7.2 0.7 all-gather.5.cloned.1.call-update
  7.9 0.7 fusion.32
  8.6 0.6 reduce-window.6
  9.4 0.8 fusion.31
  10.2 0.7 compare_select_fusion.1
  10.8 1.6 scatter_custom_fusion
  12.4 0.7 all_to_all.9
  13.1 7.6 %all-to-all-start = ((s32[16,1,32]{2,1,0:T(1,128)}), s32[16,1,32]{2,1,0:T(1,128)S(1)}, u32[]{:S(2)}, u32[]{:S(2)}) async-start(s32[16,1,32]{2,1,0:T(1,128)} %all_to_all.9), calls=%async_computation | async-start | bytes 16384 | tf_op jit(solution)/shard_map/all_to_all | solution.py:63
  20.7 3.1 scatter_custom_fusion.1
  23.7 3.3 all-to-all-done
  27.0 3.6 all-to-all-start.1
  30.7 0.5 broadcast.243
  31.2 0.7 reduce.7
  32.0 10.6 %all-to-all-done.1 = bf16[16,32,768]{2,1,0:T(8,128)(2,1)S(1)} async-done(((bf16[16,32,768]{2,1,0:T(8,128)(2,1)}), bf16[16,32,768]{2,1,0:T(8,128)(2,1)S(1)}, u32[]{:S(2)}, u32[]{:S(2)}) %all-to-all-start.1) | async-done | bytes 786464 | tf_op jit(solution)/shard_map/all_to_all | solution.py:56
  42.6 3.3 scatter_custom_fusion.2
  45.9 0.2 all-reduce.5.cloned.1.call-start
  46.2 18.8 %copy.39 = bf16[6144,3,384]{0,2,1:T(8,128)(2,1)} copy(bf16[6144,3,384]{2,0,1:T(8,128)(2,1)} %param.14) | data formatting | bytes 28311552 | tf_op args[5]
  65.1 5.2 %convolution_convert_fusion.5 = bf16[256,384]{1,0:T(8,128)(2,1)S(1)} fusion(bf16[256,6144]{1,0:T(8,128)(2,1)} %all-gather.5.cloned.1.call-done, bf16[6144,384]{1,0:T(8,128)(2,1)} %param.16), kind=kOutput, calls=%fused_computation.27 | convolution fusion | flops 1208057856 | bytes 8060928 | tf_op jit(solution)/shard_map/dot_general | solution.py:90
  70.5 5.5 %all-gather.3.cloned.1.call-done = bf16[256,6144]{1,0:T(8,128)(2,1)} async-done(((bf16[256,768]{1,0:T(8,128)(2,1)}), bf16[256,6144]{1,0:T(8,128)(2,1)}) %all-gather.3.cloned.1.call-update) | async-done | bytes 3145744 | tf_op jit(solution)/shard_map/all_gather | solution.py:73
  76.0 2.5 convert_reduce_fusion
  78.6 0.3 copy-done
  78.9 1.0 fusion.4
  79.8 7.3 %fusion.5 = f32[256,3,3,128]{0,3,2,1:T(8,128)S(1)} fusion(bf16[3,3,128,6144]{3,2,1,0:T(8,128)(2,1)} %bitcast.122, f32[6144]{0:T(1024)S(1)} %copy-done.5, bf16[256,6144]{1,0:T(8,128)(2,1)S(1)} %copy-done, f32[256]{0:T(256)S(1)} %add_rsqrt_fusion, f32[256]{0:T(256)S(1)} %broadcast_multiply_fusion.4), kind=kOutput, calls=%fused_computation.17 | convolution fusion | flops 3631742976 | bytes 18507776 | tf_op jit(solution)/shard_map/dot_general | solution.py:82
  87.4 0.5 select_reduce_fusion
  87.9 0.3 fusion.16
  88.2 0.4 multiply_reduce_fusion.1
  88.6 0.4 multiply_reduce_fusion.3
  89.0 0.4 fusion.28
  89.8 0.9 add_convert_fusion
  90.6 11.2 %fusion = bf16[256,6144]{1,0:T(8,128)(2,1)} fusion(bf16[256,3,384]{0,2,1:T(8,128)(2,1)} %bitcast.124, bf16[6144,3,384]{2,0,1:T(8,128)(2,1)} %param.14), kind=kOutput, calls=%fused_computation.8 | convolution fusion | flops 3625451520 | bytes 17891328 | tf_op jit(solution)/shard_map/dot_general | solution.py:40
  101.8 0.3 reduce-scatter.6.cloned.1.call-start
  102.1 1.5 convolution_convert_fusion.6
  103.6 5.9 %convolution_convert_fusion.2 = bf16[256,6144]{1,0:T(8,128)(2,1)} fusion(bf16[256,384]{0,1:T(8,128)(2,1)S(1)} %bitcast.129, bf16[6144,384]{1,0:T(8,128)(2,1)} %param.16), kind=kOutput, calls=%fused_computation.10 | convolution fusion | flops 1209532416 | bytes 8060928 | tf_op jit(solution)/shard_map/dot_general | solution.py:40
  109.6 5.5 %fusion.1 = bf16[6144,384]{0,1:T(8,128)(2,1)} fusion(bf16[256,384]{0,1:T(8,128)(2,1)S(1)} %bitcast.130, bf16[256,6144]{1,0:T(8,128)(2,1)} %all-gather.5.cloned.1.call-done), kind=kOutput, calls=%fused_computation.9 | convolution fusion | flops 1210318848 | bytes 8060928 | tf_op jit(solution)/shard_map/dot_general | solution.py:34
  115.1 6.7 %copy.61 = bf16[6144,384]{1,0:T(8,128)(2,1)} copy(bf16[6144,384]{0,1:T(8,128)(2,1)} %fusion.1) | data formatting | bytes 9437184
  121.9 8.9 %convolution_convert_fusion = bf16[6144,1152]{1,0:T(8,128)(2,1)} fusion(bf16[256,1152]{0,1:T(8,128)(2,1)} %bitcast.125, f32[6144]{0:T(1024)S(1)} %copy-done.5, bf16[256,6144]{1,0:T(8,128)(2,1)S(1)} %copy-done, f32[256]{0:T(256)S(1)} %add_rsqrt_fusion, f32[256]{0:T(256)S(1)} %broadcast_multiply_fusion.4), kind=kOutput, calls=%fused_computation.3 | convolution fusion | flops 3638820864 | bytes 17917952 | tf_op jit(solution)/shard_map/dot_general | solution.py:34
  130.9 38.0 %all-reduce.5.cloned.1.call-done = bf16[256,6144]{1,0:T(8,128)(2,1)} async-done(((bf16[256,6144]{1,0:T(8,128)(2,1)}), bf16[256,6144]{1,0:T(8,128)(2,1)}) %all-reduce.5.cloned.1.call-update) | async-done | bytes 3145744 | tf_op jit(solution)/shard_map/psum | solution.py:95
  168.9 4.1 %fusion.7 = (f32[256]{0:T(256)S(1)}, f32[256]{0:T(256)S(1)}, f32[256,6144]{1,0:T(8,128)S(1)}, f32[256,6144]{1,0:T(8,128)S(1)}) fusion(f32[6144]{0:T(1024)} %param.13, bf16[256,6144]{1,0:T(8,128)(2,1)} %all-reduce.5.cloned.1.call-done, f32[256]{0:T(256)S(1)} %add_rsqrt_fusion, f32[256]{0:T(256)S(1)} %broadcast_multiply_fusion.4, bf16[256,6144]{1,0:T(8,128)(2,1)S(1)} %copy-done), kind=kLoop, calls=%fused_computation.19 | loop fusion | flops 12582400 | bytes 18903040 | tf_op jit(solution)/shard_map/reduce_sum | solution.py:99
  173.1 1.0 fusion.20
  174.1 31.3 %reduce-scatter.6.cloned.1.call-done = bf16[256,768]{1,0:T(8,128)(2,1)} async-done(((bf16[256,6144]{1,0:T(8,128)(2,1)}), bf16[256,768]{1,0:T(8,128)(2,1)}) %reduce-scatter.6.cloned.1.call-update) | async-done | bytes 393232 | tf_op jit(solution)/shard_map/reduce_scatter | solution.py:86
  205.4 1.8 add_convert_fusion.1
  207.2 79.7 %reduce-scatter.10.cloned.1.call-done = bf16[384,384]{1,0:T(8,128)(2,1)} async-done(((bf16[6144,384]{1,0:T(8,128)(2,1)}), bf16[384,384]{1,0:T(8,128)(2,1)}) %reduce-scatter.10.cloned.1.call-update) | async-done | bytes 294928
  287.0 1.2 copy.62
  288.2 0.9 copy.51
  289.1 101.7 %reduce-scatter.8.cloned.1.call-done = bf16[384,1152]{1,0:T(8,128)(2,1)} async-done(((bf16[6144,1152]{1,0:T(8,128)(2,1)}), bf16[384,1152]{1,0:T(8,128)(2,1)}) %reduce-scatter.8.cloned.1.call-update) | async-done | bytes 884752 | tf_op jit(solution)/shard_map/reduce_scatter | solution.py:105
  390.8 1.3 multiply_convert_fusion.1
  392.1 0.9 copy.49
  393.0 2.2 copy.50
  (51 shorter events, 1.5 us)
Async XLA Ops:
  7.2 57.9 %all-gather.5.cloned.1.call-start = ((), (), s32[]{:S(2)}) async-start(), calls=%async_computation.7 | async-start | bytes 3538944 | tf_op jit(solution)/shard_map/all_gather | solution.py:74
  13.1 13.9 %all-to-all-start = ((s32[16,1,32]{2,1,0:T(1,128)}), s32[16,1,32]{2,1,0:T(1,128)S(1)}, u32[]{:S(2)}, u32[]{:S(2)}) async-start(s32[16,1,32]{2,1,0:T(1,128)} %all_to_all.9), calls=%async_computation | async-start | bytes 16384 | tf_op jit(solution)/shard_map/all_to_all | solution.py:63
  27.0 15.6 %all-to-all-start.1 = ((bf16[16,32,768]{2,1,0:T(8,128)(2,1)}), bf16[16,32,768]{2,1,0:T(8,128)(2,1)S(1)}, u32[]{:S(2)}, u32[]{:S(2)}) async-start(bf16[16,32,768]{2,1,0:T(8,128)(2,1)} %bitcast.3), calls=%async_computation.1 | async-start | bytes 1572864 | tf_op jit(solution)/shard_map/all_to_all | solution.py:56
  30.6 45.4 %all-gather.3.cloned.1.call-start = ((), (), s32[]{:S(2)}) async-start(), calls=%async_computation.5 | async-start | bytes 3538944 | tf_op jit(solution)/shard_map/all_gather | solution.py:73
  45.9 19.0 %copy-start.7 = (f32[2,128]{1,0:T(2,128)S(1)}, f32[2,128]{1,0:T(2,128)}, u32[]{:S(2)}) copy-start(f32[2,128]{1,0:T(2,128)} %param.15) | copy-start | bytes 3076
  45.9 19.0 %copy-start.6 = (s32[256]{0:T(256)S(1)}, s32[256]{0:T(256)}, u32[]{:S(2)}) copy-start(s32[256]{0:T(256)} %param.12) | copy-start | bytes 3076
  45.9 123.0 %all-reduce.5.cloned.1.call-start = ((), (), s32[]{:S(2)}) async-start(), calls=%async_computation.8 | async-start | bytes 6291456 | tf_op jit(solution)/shard_map/psum | solution.py:95
  70.3 9.5 %copy-start.5 = (f32[6144]{0:T(1024)S(1)}, f32[6144]{0:T(1024)}, u32[]{:S(2)}) copy-start(f32[6144]{0:T(1024)} %param.13) | copy-start | bytes 73732
  76.0 2.8 copy-start
  87.2 2.5 copy-start.1
  87.9 1.1 copy-start.4
  101.8 103.6 %reduce-scatter.6.cloned.1.call-start = ((), (), s32[]{:S(2)}) async-start(), calls=%async_computation.6 | async-start | bytes 3538944 | tf_op jit(solution)/shard_map/reduce_scatter | solution.py:86
  109.6 177.4 %reduce-scatter.10.cloned.1.call-start = ((), (), s32[]{:S(2)}) async-start(), calls=%async_computation.10 | async-start | bytes 5013504
  121.9 268.9 %reduce-scatter.8.cloned.1.call-start = ((), (), s32[]{:S(2)}) async-start(), calls=%async_computation.9 | async-start | bytes 15040512 | tf_op jit(solution)/shard_map/reduce_scatter | solution.py:105
  130.9 74.5 %copy-start.2 = (bf16[256,768]{1,0:T(8,128)(2,1)S(1)}, bf16[256,768]{1,0:T(8,128)(2,1)}, u32[]{:S(2)}) copy-start(bf16[256,768]{1,0:T(8,128)(2,1)} %scatter_custom_fusion.2) | copy-start | bytes 1179652
  168.9 4.2 %copy-start.3 = (bf16[256,768]{1,0:T(8,128)(2,1)S(1)}, bf16[256,768]{1,0:T(8,128)(2,1)}, u32[]{:S(2)}) copy-start(bf16[256,768]{1,0:T(8,128)(2,1)} %param.17) | copy-start | bytes 1179652
Sparse Core Ops, SparseCore 0:
  9.7 31.5 all-gather.4
  46.0 29.9 all-gather.2
  102.0 66.9 all-reduce.4
  171.2 34.1 reduce-scatter.5
  208.6 78.3 reduce-scatter.9
  290.3 100.3 reduce-scatter.7
where the time goes:
time: 403 us; the launch traced here: 402 us
  waiting for transfers between devices  271 us (67%)
  matrix products  47.5 us (12%)
  local copies, waits for them, and re-layouts  40.4 us (10%)
  other arithmetic  16.8 us (4%)
  between operations  14.4 us (4%)
  starting transfers between devices  11.8 us (3%)
    reduce_scatter x1, waiting for transfers between devices, shards(): lax.psum_scatter(contract_rows(normed, d_proj_bf).astype(jnp.bfloat16), '...  102 us
    unnamed x7, waiting for transfers between devices  80.5 us
    psum x1, waiting for transfers between devices, shards(): d_normed = lax.psum(d_part.astype(jnp.bfloat16), 'mp').astype(jnp.float32)  38 us
    reduce_scatter x1, waiting for transfers between devices, shards(): lax.psum_scatter(contract_cols(heads_out, w_out).astype(jnp.bfloat16), 'm...  31.3 us
    unnamed x21, local copies, waits for them, and re-layouts  30 us
    dot_general x2, matrix products, contract_cols(): lax.dot_general(left, right, (((1,), (1,)), ((), ())), preferred_element_...  17.1 us
    dot_general x2, matrix products, contract_rows(): lax.dot_general(left, right, (((0,), (0,)), ((), ())), preferred_element_...  14.4 us
    all_to_all x1, waiting for transfers between devices, shards(): lax.all_to_all(outbox.reshape(groups, slot_size, part_width), 'dp', split...  10.6 us
  transfers between devices with their start and end apart: 8, of which 7 were waited for; matrix products, arithmetic and copies ran while one was open for 18% of the time, Pallas kernels for 0%

commit v1 on v0

--- a/solution.py
+++ b/solution.py
@@ -92,7 +92,9 @@
     d_proj_bf = d_projected.astype(jnp.bfloat16).reshape(group_rows, 3 * local_width)
     d_part = contract_cols(d_proj_bf, w_flat)
     my_index = lax.axis_index("mp")
-    d_normed = lax.psum(d_part.astype(jnp.bfloat16), "mp").astype(jnp.float32)
+    d_normed = jnp.sum(lax.all_gather(d_part.astype(jnp.bfloat16), "mp"), axis=0).astype(
+        jnp.float32
+    )
     d_unit = d_normed * ln_gain
     d_full = rstd * (
         d_unit

time: 403 us -> 476 us (1.18)
  waiting for transfers between devices: 271 us -> 323 us
  other arithmetic: 16.8 us -> 33.4 us
    all_gather x0 -> x1, waiting for transfers between devices: none -> 115 us  [shards(): lax.all_gather(d_part.astype(jnp.bfloat16), 'mp')]
    psum x1 -> x0, waiting for transfers between devices: 38 us -> none  [shards(): d_normed = lax.psum(d_part.astype(jnp.bfloat16), 'mp').astype(jnp.float32)]
    reduce_scatter x1, waiting for transfers between devices: 31.3 us -> 0.02 us  [shards(): lax.psum_scatter(contract_cols(heads_out, w_out).astype(jnp.bfloat16), 'm...]
    reduce_sum x0 -> x1, other arithmetic: none -> 15.8 us  [shards(): jnp.sum(lax.all_gather(d_part.astype(jnp.bfloat16), 'mp'), axis=0)]
    all_gather x1, waiting for transfers between devices: 0.02 us -> 13 us  [shards(): lax.all_gather(cotangent, 'mp', axis=1, tiled=True)]
    unnamed x7, waiting for transfers between devices: 80.5 us -> 71.1 us
    all_gather x1, waiting for transfers between devices: 5.52 us -> 10.3 us  [shards(): lax.all_gather(packed, 'mp', axis=1, tiled=True)]
    unnamed x21 -> x33, local copies, waits for them, and re-layouts: 30 us -> 32.4 us
  transfers between devices with their start and end apart: 8 -> 8, of which waited for: 7 -> 7; matrix products, arithmetic and copies ran while one was open for 18% -> 20% of each run, Pallas kernels for 0% -> 0%
where the time goes in v1:
time: 476 us; the launch traced here: 475 us
  waiting for transfers between devices  323 us (68%)
  matrix products  46.4 us (10%)
  local copies, waits for them, and re-layouts  45.1 us (9%)
  other arithmetic  33.4 us (7%)
  between operations  14.4 us (3%)
  starting transfers between devices  12.1 us (3%)
    all_gather x1, waiting for transfers between devices, shards(): lax.all_gather(d_part.astype(jnp.bfloat16), 'mp')  115 us
    reduce_scatter x1, waiting for transfers between devices, shards(): lax.psum_scatter(contract_rows(normed, d_proj_bf).astype(jnp.bfloat16), '...  100 us
    unnamed x7, waiting for transfers between devices  71.1 us
    unnamed x33, local copies, waits for them, and re-layouts  32.4 us
    reduce_sum x1, other arithmetic, shards(): jnp.sum(lax.all_gather(d_part.astype(jnp.bfloat16), 'mp'), axis=0)  15.8 us
    dot_general x2, matrix products, contract_cols(): lax.dot_general(left, right, (((1,), (1,)), ((), ())), preferred_element_...  14.8 us
    dot_general x2, matrix products, contract_rows(): lax.dot_general(left, right, (((0,), (0,)), ((), ())), preferred_element_...  13.3 us
    all_gather x1, waiting for transfers between devices, shards(): lax.all_gather(cotangent, 'mp', axis=1, tiled=True)  13 us
  transfers between devices with their start and end apart: 8, of which 7 were waited for; matrix products, arithmetic and copies ran while one was open for 20% of the time, Pallas kernels for 0%

profile of v1, /device:TPU:1, one launch (start us, length us, event | category | flops | bytes accessed | tf_op | source)
XLA Modules:
  0.0 474.7 jit_solution(1662176876880027350)
XLA Ops:
  7.2 0.7 fusion.32
  7.9 0.6 reduce-window.6
  8.6 0.8 fusion.31
  9.4 0.7 compare_select_fusion.1
  10.1 1.6 scatter_custom_fusion
  11.7 0.7 all_to_all.9
  12.3 7.6 %all-to-all-start = ((s32[16,1,32]{2,1,0:T(1,128)}), s32[16,1,32]{2,1,0:T(1,128)S(1)}, u32[]{:S(2)}, u32[]{:S(2)}) async-start(s32[16,1,32]{2,1,0:T(1,128)} %all_to_all.9), calls=%async_computation | async-start | bytes 16384 | tf_op jit(solution)/shard_map/all_to_all | solution.py:63
  19.9 3.0 scatter_custom_fusion.1
  23.0 3.3 all-to-all-done
  26.3 3.6 all-to-all-start.1
  29.9 0.5 broadcast.243
  30.5 0.7 reduce.8
  31.2 10.6 %all-to-all-done.1 = bf16[16,32,768]{2,1,0:T(8,128)(2,1)S(1)} async-done(((bf16[16,32,768]{2,1,0:T(8,128)(2,1)}), bf16[16,32,768]{2,1,0:T(8,128)(2,1)S(1)}, u32[]{:S(2)}, u32[]{:S(2)}) %all-to-all-start.1) | async-done | bytes 786464 | tf_op jit(solution)/shard_map/all_to_all | solution.py:56
  41.8 3.3 scatter_custom_fusion.2
  45.2 0.7 all-gather.7.cloned.1.call-update
  46.2 18.6 %copy.39 = bf16[6144,3,384]{0,2,1:T(8,128)(2,1)} copy(bf16[6144,3,384]{2,0,1:T(8,128)(2,1)} %param.14) | data formatting | bytes 28311552 | tf_op args[5]
  65.0 10.3 %all-gather.5.cloned.1.call-done = bf16[256,6144]{1,0:T(8,128)(2,1)} async-done(((bf16[256,768]{1,0:T(8,128)(2,1)}), bf16[256,6144]{1,0:T(8,128)(2,1)}) %all-gather.5.cloned.1.call-update) | async-done | bytes 3145744 | tf_op jit(solution)/shard_map/all_gather | solution.py:73
  75.3 2.5 convert_reduce_fusion
  78.1 1.0 fusion.4
  79.1 7.5 %fusion.5 = f32[256,3,3,128]{0,3,2,1:T(8,128)S(1)} fusion(bf16[3,3,128,6144]{3,2,1,0:T(8,128)(2,1)} %bitcast.124, f32[6144]{0:T(1024)S(1)} %copy-done.8, bf16[256,6144]{1,0:T(8,128)(2,1)S(1)} %copy-done, f32[256]{0:T(256)S(1)} %add_rsqrt_fusion, f32[256]{0:T(256)S(1)} %broadcast_multiply_fusion.4), kind=kOutput, calls=%fused_computation.17 | convolution fusion | flops 3631742976 | bytes 18507776 | tf_op jit(solution)/shard_map/dot_general | solution.py:82
  86.8 0.5 select_reduce_fusion
  87.3 0.4 copy-done.1
  88.2 3.6 convolution_convert_fusion.2
  91.8 13.0 %all-gather.7.cloned.1.call-done = bf16[256,6144]{1,0:T(8,128)(2,1)} async-done(((bf16[256,768]{1,0:T(8,128)(2,1)}), bf16[256,6144]{1,0:T(8,128)(2,1)}) %all-gather.7.cloned.1.call-update) | async-done | bytes 3145744 | tf_op jit(solution)/shard_map/all_gather | solution.py:74
  104.9 5.4 %fusion.1 = bf16[6144,384]{0,1:T(8,128)(2,1)} fusion(bf16[256,384]{0,1:T(8,128)(2,1)S(1)} %bitcast.134, bf16[256,6144]{1,0:T(8,128)(2,1)} %all-gather.7.cloned.1.call-done), kind=kOutput, calls=%fused_computation.9 | convolution fusion | flops 1210318848 | bytes 8060928 | tf_op jit(solution)/shard_map/dot_general | solution.py:34
  110.3 6.7 %copy.61 = bf16[6144,384]{1,0:T(8,128)(2,1)} copy(bf16[6144,384]{0,1:T(8,128)(2,1)} %fusion.1) | data formatting | bytes 9437184
  117.3 5.8 %convolution_convert_fusion.5 = bf16[256,384]{1,0:T(8,128)(2,1)} fusion(bf16[256,6144]{1,0:T(8,128)(2,1)} %all-gather.7.cloned.1.call-done, bf16[6144,384]{1,0:T(8,128)(2,1)} %param.16), kind=kOutput, calls=%fused_computation.27 | convolution fusion | flops 1208057856 | bytes 8060928 | tf_op jit(solution)/shard_map/dot_general | solution.py:90
  123.1 1.1 copy.43
  124.2 1.8 multiply_reduce_fusion.1
  126.0 1.8 multiply_reduce_fusion.3
  127.8 0.4 fusion.28
  128.9 0.8 copy-done.4
  129.7 7.8 %convolution_convert_fusion = bf16[6144,1152]{1,0:T(8,128)(2,1)} fusion(bf16[256,1152]{0,1:T(8,128)(2,1)S(1)} %bitcast.128, f32[6144]{0:T(1024)S(1)} %copy-done.8, bf16[256,6144]{1,0:T(8,128)(2,1)S(1)} %copy-done, f32[256]{0:T(256)S(1)} %add_rsqrt_fusion, f32[256]{0:T(256)S(1)} %broadcast_multiply_fusion.4), kind=kOutput, calls=%fused_computation.3 | convolution fusion | flops 3638820864 | bytes 17917952 | tf_op jit(solution)/shard_map/dot_general | solution.py:34
  137.6 0.3 all-gather.9.cloned.1.call-start
  137.9 11.3 %fusion = bf16[256,6144]{1,0:T(8,128)(2,1)} fusion(bf16[256,3,384]{0,2,1:T(8,128)(2,1)} %bitcast.129, bf16[6144,3,384]{2,0,1:T(8,128)(2,1)} %param.14), kind=kOutput, calls=%fused_computation.8 | convolution fusion | flops 3625451520 | bytes 17891328 | tf_op jit(solution)/shard_map/dot_general | solution.py:40
  149.3 1.8 add_convert_fusion.1
  151.1 70.3 %reduce-scatter.10.cloned.1.call-done = bf16[384,384]{1,0:T(8,128)(2,1)} async-done(((bf16[6144,384]{1,0:T(8,128)(2,1)}), bf16[384,384]{1,0:T(8,128)(2,1)}) %reduce-scatter.10.cloned.1.call-update) | async-done | bytes 294928
  221.4 1.2 copy.62
  222.6 0.8 multiply_convert_fusion.4
  223.4 1.8 copy.51
  225.2 100.1 %reduce-scatter.8.cloned.1.call-done = bf16[384,1152]{1,0:T(8,128)(2,1)} async-done(((bf16[6144,1152]{1,0:T(8,128)(2,1)}), bf16[384,1152]{1,0:T(8,128)(2,1)}) %reduce-scatter.8.cloned.1.call-update) | async-done | bytes 884752 | tf_op jit(solution)/shard_map/reduce_scatter | solution.py:107
  325.3 2.2 multiply_convert_fusion.1
  327.5 2.3 copy.49
  329.8 2.3 copy.50
  332.1 114.8 %all-gather.9.cloned.1.call-done = bf16[2048,6144]{1,0:T(8,128)(2,1)} async-done(((bf16[256,6144]{1,0:T(8,128)(2,1)}), bf16[2048,6144]{1,0:T(8,128)(2,1)}) %all-gather.9.cloned.1.call-update) | async-done | bytes 25165840 | tf_op jit(solution)/shard_map/all_gather | solution.py:95
  446.9 15.8 %reduce_sum.180 = bf16[256,6144]{1,0:T(8,128)(2,1)} reduce(bf16[8,256,6144]{2,1,0:T(8,128)(2,1)} %bitcast.123, bf16[]{:T(256)} %constant.20.clone.1), dimensions={0}, to_apply=%region_19.20 | reduce | flops 11010048 | bytes 28311554 | tf_op jit(solution)/shard_map/reduce_sum | solution.py:95
  462.7 4.1 fusion.7
  466.9 1.0 fusion.20
  (65 shorter events, 2.9 us)
Async XLA Ops:
  12.3 13.9 %all-to-all-start = ((s32[16,1,32]{2,1,0:T(1,128)}), s32[16,1,32]{2,1,0:T(1,128)S(1)}, u32[]{:S(2)}, u32[]{:S(2)}) async-start(s32[16,1,32]{2,1,0:T(1,128)} %all_to_all.9), calls=%async_computation | async-start | bytes 16384 | tf_op jit(solution)/shard_map/all_to_all | solution.py:63
  26.3 15.6 %all-to-all-start.1 = ((bf16[16,32,768]{2,1,0:T(8,128)(2,1)}), bf16[16,32,768]{2,1,0:T(8,128)(2,1)S(1)}, u32[]{:S(2)}, u32[]{:S(2)}) async-start(bf16[16,32,768]{2,1,0:T(8,128)(2,1)} %bitcast.3), calls=%async_computation.1 | async-start | bytes 1572864 | tf_op jit(solution)/shard_map/all_to_all | solution.py:56
  29.9 45.4 %all-gather.5.cloned.1.call-start = ((), (), s32[]{:S(2)}) async-start(), calls=%async_computation.5 | async-start | bytes 3538944 | tf_op jit(solution)/shard_map/all_gather | solution.py:73
  45.2 59.7 %all-gather.7.cloned.1.call-start = ((), (), s32[]{:S(2)}) async-start(), calls=%async_computation.7 | async-start | bytes 3538944 | tf_op jit(solution)/shard_map/all_gather | solution.py:74
  45.9 18.9 %copy-start.11 = (f32[2,128]{1,0:T(2,128)S(1)}, f32[2,128]{1,0:T(2,128)}, u32[]{:S(2)}) copy-start(f32[2,128]{1,0:T(2,128)} %param.15) | copy-start | bytes 3076
  46.0 18.9 %copy-start.10 = (s32[256]{0:T(256)S(1)}, s32[256]{0:T(256)}, u32[]{:S(2)}) copy-start(s32[256]{0:T(256)} %param.12) | copy-start | bytes 3076
  46.0 103.3 %reduce-scatter.6.cloned.1.call-start = ((), (), s32[]{:S(2)}) async-start(), calls=%async_computation.6 | async-start | bytes 3538944 | tf_op jit(solution)/shard_map/reduce_scatter | solution.py:86
  64.8 14.3 %copy-start.8 = (f32[6144]{0:T(1024)S(1)}, f32[6144]{0:T(1024)}, u32[]{:S(2)}) copy-start(f32[6144]{0:T(1024)} %param.13) | copy-start | bytes 73732
  75.3 2.8 copy-start
  79.1 9.1 %slice-start = ((s8[4718592]{0:T(1024)(128)(4,1)}), s8[4194304]{0:T(1024)(128)(4,1)S(1)}, s32[]{:S(2)}) async-start(s8[4718592]{0:T(1024)(128)(4,1)} %bitcast.125), calls=%async_computation.11 | async-start | bytes 8388608
  79.1 9.1 %slice-start.1 = ((s8[4718592]{0:T(1024)(128)(4,1)}), s8[524288]{0:T(1024)(128)(4,1)S(1)}, s32[]{:S(2)}) async-start(s8[4718592]{0:T(1024)(128)(4,1)} %bitcast.125), calls=%async_computation.12 | async-start | bytes 1048576
  86.6 1.1 copy-start.1
  87.3 0.9 copy-start.6
  91.8 129.6 %reduce-scatter.10.cloned.1.call-start = ((), (), s32[]{:S(2)}) async-start(), calls=%async_computation.10 | async-start | bytes 5013504
  117.0 208.3 %reduce-scatter.8.cloned.1.call-start = ((), (), s32[]{:S(2)}) async-start(), calls=%async_computation.8 | async-start | bytes 15040512 | tf_op jit(solution)/shard_map/reduce_scatter | solution.py:107
  124.2 3.6 copy-start.2
  124.2 3.6 copy-start.7
  128.9 0.8 copy-start.4
  137.6 309.3 %all-gather.9.cloned.1.call-start = ((), (), s32[]{:S(2)}) async-start(), calls=%async_computation.9 | async-start | bytes 28311552 | tf_op jit(solution)/shard_map/all_gather | solution.py:95
  137.9 11.3 %copy-start.3 = (bf16[256,768]{1,0:T(8,128)(2,1)S(1)}, bf16[256,768]{1,0:T(8,128)(2,1)}, u32[]{:S(2)}) copy-start(bf16[256,768]{1,0:T(8,128)(2,1)} %scatter_custom_fusion.2) | copy-start | bytes 1179652
  446.9 15.8 %copy-start.9 = (f32[6144]{0:T(1024)S(1)}, f32[6144]{0:T(1024)}, u32[]{:S(2)}) copy-start(f32[6144]{0:T(1024)} %param.13) | copy-start | bytes 73732
  462.7 4.2 copy-start.5
Sparse Core Ops, SparseCore 0:
  45.3 29.9 all-gather.4
  77.0 27.8 all-gather.6
  107.3 32.1 reduce-scatter.5
  142.7 78.7 reduce-scatter.9
  224.8 100.4 reduce-scatter.7
  327.0 119.8 all-gather.8
